TPU v7x, 256 devices: a whole 4x4x8 slice. The times are simulated.
256 devices in a mesh: ctx: 64 (over z, x, core), kvh: 4 (over y).
Axes of the slice: x: 4, y: 4, z: 8, core: 2. Of those that a mesh axis runs over, the one named last changes fastest.
Arguments:
- query_act: bfloat16 [16384, 8192], P(('ctx', 'kvh')), may hold values from -6 to 6
- key_act: bfloat16 [16384, 1024], P(('ctx', 'kvh')), may hold values from -6 to 6
- value_act: bfloat16 [16384, 1024], P(('ctx', 'kvh')), may hold values from -6 to 6
- grad_out: bfloat16 [16384, 8192], P(('ctx', 'kvh')), may hold values from -6 to 6
Outputs:
- attn_out: bfloat16 [16384, 8192], P(('ctx', 'kvh'))
- grad_query: bfloat16 [16384, 8192], P(('ctx', 'kvh'))
- grad_key: bfloat16 [16384, 1024], P(('ctx', 'kvh'))
- grad_value: bfloat16 [16384, 1024], P(('ctx', 'kvh'))
All inputs are finite; a program needn't handle non-finite values.
Results may differ from a plain program's by a relative error of at most 0.014.
Values may be sent and summed in bfloat16 or wider, within the bound.
A program may use at most 128 MiB of HBM per device.

v0:
```python
import jax
import jax.numpy as jnp
from jax import lax
from jax.experimental import pallas as pl
from jax.experimental.pallas import tpu as pltpu
from jax.sharding import PartitionSpec as P

HD = 128
QPK = 8
BLK = 256
NL = 7
SCALE = HD**-0.5
C2 = SCALE * 1.4426950408889634
F32 = jnp.float32
BF = jnp.bfloat16
GRP = 2


def nt(a, b):
    return lax.dot_general(a, b, (((1,), (1,)), ((), ())), preferred_element_type=F32)


def nn(a, b):
    return lax.dot_general(a, b, (((1,), (0,)), ((), ())), preferred_element_type=F32)


def head(g, r, valid, q_ref, g_ref, kv, kt_ref, vt_ref, out_ref, gq_ref, s_scr, dp_scr, p_scr, ds_scr, gs_scr, qs_scr):
    col = pl.multiple_of((g * QPK + r) * HD, HD)
    row = pl.multiple_of(r * BLK, BLK)
    q = q_ref[:, pl.ds(col, HD)]
    go = g_ref[:, pl.ds(col, HD)]
    kc = slice(g * HD, (g + 1) * HD)
    vc = slice((GRP + g) * HD, (GRP + g + 1) * HD)
    top = None
    for j in range(NL):
        s = nt(kv[j][:, kc], q)
        dp_scr[j] = nt(kv[j][:, vc], go)
        if j == 0:
            u = lax.broadcasted_iota(jnp.int32, (BLK, BLK), 0)
            t = lax.broadcasted_iota(jnp.int32, (BLK, BLK), 1)
            s = jnp.where(u <= t, s, -1e30)
        s_scr[j] = s
        mj = jnp.max(s, axis=0, keepdims=True)
        top = mj if j == 0 else jnp.maximum(top, jnp.where(valid[j], mj, -1e30))
    total = jnp.zeros((1, BLK), F32)
    acc = jnp.zeros((HD, BLK), F32)
    for j in range(NL):
        sub = top if j == 0 else jnp.where(valid[j], top, 1e30)
        p = jnp.exp2((s_scr[j] - sub) * C2)
        s_scr[j] = p
        total = total + jnp.sum(p, axis=0, keepdims=True)
        pb = p.astype(BF)
        p_scr[j, :, pl.ds(row, BLK)] = pb
        acc = acc + nn(vt_ref[j, g], pb)
    inv = 1.0 / total
    ot = (acc * inv).astype(BF)
    out_ref[:, pl.ds(col, HD)] = ot.T
    delta = jnp.sum(ot.astype(F32) * go.T.astype(F32), axis=0, keepdims=True)
    acc = jnp.zeros((HD, BLK), F32)
    for j in range(NL):
        ds = (s_scr[j] * (dp_scr[j] - delta)).astype(BF)
        ds_scr[j, :, pl.ds(row, BLK)] = ds
        acc = acc + nn(kt_ref[j, g], ds)
    gq_ref[:, pl.ds(col, HD)] = (acc * (inv * SCALE)).astype(BF).T
    invb = jnp.broadcast_to(inv, (HD, BLK)).T
    gs_scr[pl.ds(row, BLK), :] = (go.astype(F32) * invb).astype(BF)
    qs_scr[pl.ds(row, BLK), :] = (q.astype(F32) * (invb * SCALE)).astype(BF)


def kernel(*refs):
    q_ref, g_ref = refs[:2]
    kv = refs[2 : 2 + NL]
    out_ref, gq_ref = refs[9:11]
    gkv = refs[11 : 11 + NL]
    kt_ref, vt_ref, s_scr, dp_scr, p_scr, ds_scr, gs_scr, qs_scr = refs[18:]
    ctx = lax.axis_index("ctx")
    valid = [None] + [ctx >= 1 << j for j in range(NL - 1)]
    for g in range(GRP):
        kc = slice(g * HD, (g + 1) * HD)
        vc = slice((GRP + g) * HD, (GRP + g + 1) * HD)
        for j in range(NL):
            kt_ref[j, g] = kv[j][:, kc].T
            vt_ref[j, g] = kv[j][:, vc].T

        def body(r, _):
            head(g, r, valid, q_ref, g_ref, kv, kt_ref, vt_ref, out_ref, gq_ref, s_scr, dp_scr, p_scr, ds_scr, gs_scr, qs_scr)
            return 0

        lax.fori_loop(0, QPK, body, 0)
        for j in range(NL):
            gkv[j][:, vc] = nn(p_scr[j], gs_scr[...]).astype(BF)
            gkv[j][:, kc] = nn(ds_scr[j], qs_scr[...]).astype(BF)


VM = pl.BlockSpec(memory_space=pltpu.VMEM)


def shifted(array, by):
    peers = lax.axis_size("ctx")
    return lax.ppermute(array, "ctx", [(i, i + by) for i in range(peers) if 0 <= i + by < peers])


def a2a_in(x):
    return lax.all_to_all(x, "kvh", split_axis=1, concat_axis=0, tiled=True)


def a2a_out(x):
    return lax.all_to_all(x, "kvh", split_axis=0, concat_axis=1, tiled=True)


def shards(query_act, key_act, value_act, grad_out):
    tok = query_act.shape[0]
    kv_loc = jnp.concatenate([key_act.reshape(tok, 4, -1), value_act.reshape(tok, 4, -1)], 2).reshape(tok, -1)
    own = a2a_in(kv_loc)
    kv = [own] + [shifted(own, 1 << j) for j in range(NL - 1)]
    q = a2a_in(query_act)
    go = a2a_in(grad_out)
    res = pl.pallas_call(
        kernel,
        out_shape=(jax.ShapeDtypeStruct((BLK, GRP * QPK * HD), BF),) * 2
        + (jax.ShapeDtypeStruct((BLK, 2 * GRP * HD), BF),) * NL,
        in_specs=[VM] * (2 + NL),
        out_specs=(VM,) * (2 + NL),
        scratch_shapes=[pltpu.VMEM((NL, GRP, HD, BLK), BF)] * 2
        + [pltpu.VMEM((NL, BLK, BLK), F32)] * 2
        + [pltpu.VMEM((NL, BLK, QPK * BLK), BF)] * 2
        + [pltpu.VMEM((QPK * BLK, HD), BF)] * 2,
        compiler_params=pltpu.CompilerParams(vmem_limit_bytes=56 * 2**20),
    )(q, go, *kv)
    out, gq = res[:2]
    gkv = res[2:]
    total = gkv[0].astype(F32)
    for j in range(NL - 1):
        total = total + shifted(gkv[1 + j], -(1 << j)).astype(F32)
    back = a2a_out(total.astype(BF)).reshape(tok, 4, 2, -1)
    return (
        a2a_out(out),
        a2a_out(gq),
        back[:, :, 0].reshape(tok, -1),
        back[:, :, 1].reshape(tok, -1),
    )


def solution(mesh):
    spec = P(("ctx", "kvh"), None)
    return jax.shard_map(shards, mesh=mesh, in_specs=(spec,) * 4, out_specs=(spec,) * 4, check_vma=False)
```

profile of v0, /device:TPU:64, one launch (start us, length us, event | category | flops | bytes accessed | tf_op | source)
XLA Modules:
  0.0 222.7 jit_solution(1039269577168742142)
XLA Ops:
  0.6 0.0 copy-start.2
  0.6 1.1 copy_bitcast_fusion.2
  1.7 0.7 pad_maximum_fusion
  2.4 4.5 %all-to-all-start.2 = ((bf16[64,4,512]{2,0,1:T(8,128)(2,1)}), bf16[64,4,512]{2,0,1:T(8,128)(2,1)S(1)}, u32[]{:S(2)}, u32[]{:S(2)}) async-start(bf16[64,4,512]{2,0,1:T(8,128)(2,1)} %pad_maximum_fusion), calls=%async_computation.2 | async-start | bytes 524288 | tf_op jit(solution)/shard_map/all_to_all | solution.py:104
  6.9 0.0 copy-done.2
  6.9 1.0 copy.31
  7.9 5.6 %all-to-all-done.2 = bf16[64,4,512]{2,0,1:T(8,128)(2,1)S(1)} async-done(((bf16[64,4,512]{2,0,1:T(8,128)(2,1)}), bf16[64,4,512]{2,0,1:T(8,128)(2,1)S(1)}, u32[]{:S(2)}, u32[]{:S(2)}) %all-to-all-start.2) | async-done | bytes 262176 | tf_op jit(solution)/shard_map/all_to_all | solution.py:104
  13.6 0.0 copy-start.5
  13.6 0.0 copy-start.3
  13.6 3.6 %all-to-all-start = ((bf16[64,4,2048]{2,0,1:T(8,128)(2,1)}), bf16[64,4,2048]{2,0,1:T(8,128)(2,1)S(1)}, u32[]{:S(2)}, u32[]{:S(2)}) async-start(bf16[64,4,2048]{2,0,1:T(8,128)(2,1)} %bitcast.42), calls=%async_computation | async-start | bytes 2097152 | tf_op jit(solution)/shard_map/all_to_all | solution.py:104
  17.2 0.0 copy-done.3
  17.3 1.0 copy.30
  18.3 12.9 %all-to-all-done = bf16[64,4,2048]{2,0,1:T(8,128)(2,1)S(1)} async-done(((bf16[64,4,2048]{2,0,1:T(8,128)(2,1)}), bf16[64,4,2048]{2,0,1:T(8,128)(2,1)S(1)}, u32[]{:S(2)}, u32[]{:S(2)}) %all-to-all-start) | async-done | bytes 1048608 | tf_op jit(solution)/shard_map/all_to_all | solution.py:104
  31.2 0.0 copy-start
  31.2 1.0 copy-done
  32.2 3.5 %all-to-all-start.1 = ((bf16[64,4,2048]{2,0,1:T(8,128)(2,1)}), bf16[64,4,2048]{2,0,1:T(8,128)(2,1)S(1)}, u32[]{:S(2)}, u32[]{:S(2)}) async-start(bf16[64,4,2048]{2,0,1:T(8,128)(2,1)} %bitcast.41), calls=%async_computation.1 | async-start | bytes 2097152 | tf_op jit(solution)/shard_map/all_to_all | solution.py:104
  35.7 7.3 %collective-permute-start.5 = (bf16[256,512]{1,0:T(8,128)(2,1)S(1)}, bf16[256,512]{1,0:T(8,128)(2,1)S(1)}, u32[]{:S(2)}, u32[]{:S(2)}) collective-permute-start(bf16[256,512]{1,0:T(8,128)(2,1)S(1)} %bitcast.54), channel_id=1, source_target_pairs={{0,128},{4,132},{8,136},{12,140},{16,144},{20,148},{24,152},{28,15... | collective-permute-start | bytes 786440 | tf_op jit(solution)/shard_map/ppermute | solution.py:100
  43.0 1.9 collective-permute-start.4
  44.9 2.9 %collective-permute-start.3 = (bf16[256,512]{1,0:T(8,128)(2,1)S(1)}, bf16[256,512]{1,0:T(8,128)(2,1)S(1)}, u32[]{:S(2)}, u32[]{:S(2)}) collective-permute-start(bf16[256,512]{1,0:T(8,128)(2,1)S(1)} %bitcast.56), channel_id=1, source_target_pairs={{0,32},{4,36},{8,40},{12,44},{16,48},{20,52},{24,56},{28,60},{32,6... | collective-permute-start | bytes 786440 | tf_op jit(solution)/shard_map/ppermute | solution.py:100
  47.9 4.9 %collective-permute-start.2 = (bf16[256,512]{1,0:T(8,128)(2,1)S(1)}, bf16[256,512]{1,0:T(8,128)(2,1)S(1)}, u32[]{:S(2)}, u32[]{:S(2)}) collective-permute-start(bf16[256,512]{1,0:T(8,128)(2,1)S(1)} %bitcast.57), channel_id=1, source_target_pairs={{0,16},{4,20},{8,24},{12,28},{16,32},{20,36},{24,40},{28,44},{32,4... | collective-permute-start | bytes 786440 | tf_op jit(solution)/shard_map/ppermute | solution.py:100
  52.8 2.5 %collective-permute-start.1 = (bf16[256,512]{1,0:T(8,128)(2,1)S(1)}, bf16[256,512]{1,0:T(8,128)(2,1)S(1)}, u32[]{:S(2)}, u32[]{:S(2)}) collective-permute-start(bf16[256,512]{1,0:T(8,128)(2,1)S(1)} %bitcast.58), channel_id=1, source_target_pairs={{0,8},{4,12},{8,16},{12,20},{16,24},{20,28},{24,32},{28,36},{32,40... | collective-permute-start | bytes 786440 | tf_op jit(solution)/shard_map/ppermute | solution.py:100
  55.3 0.5 collective-permute-done.5.refs_8_
  55.8 0.0 copy-done.5
  55.8 1.9 collective-permute-start
  57.8 6.4 %collective-permute-done.4.refs_7_ = bf16[256,512]{1,0:T(8,128)(2,1)S(1)} collective-permute-done((bf16[256,512]{1,0:T(8,128)(2,1)S(1)}, bf16[256,512]{1,0:T(8,128)(2,1)S(1)}, u32[]{:S(2)}, u32[]{:S(2)}) %collective-permute-start.4) | collective-permute-done | bytes 262176 | tf_op jit(solution)/shard_map/ppermute | solution.py:100
  64.2 4.6 %collective-permute-done.3.refs_6_ = bf16[256,512]{1,0:T(8,128)(2,1)S(1)} collective-permute-done((bf16[256,512]{1,0:T(8,128)(2,1)S(1)}, bf16[256,512]{1,0:T(8,128)(2,1)S(1)}, u32[]{:S(2)}, u32[]{:S(2)}) %collective-permute-start.3) | collective-permute-done | bytes 262176 | tf_op jit(solution)/shard_map/ppermute | solution.py:100
  68.8 4.6 %collective-permute-done.2.refs_5_ = bf16[256,512]{1,0:T(8,128)(2,1)S(1)} collective-permute-done((bf16[256,512]{1,0:T(8,128)(2,1)S(1)}, bf16[256,512]{1,0:T(8,128)(2,1)S(1)}, u32[]{:S(2)}, u32[]{:S(2)}) %collective-permute-start.2) | collective-permute-done | bytes 262176 | tf_op jit(solution)/shard_map/ppermute | solution.py:100
  73.4 5.6 %collective-permute-done.1.refs_4_ = bf16[256,512]{1,0:T(8,128)(2,1)S(1)} collective-permute-done((bf16[256,512]{1,0:T(8,128)(2,1)S(1)}, bf16[256,512]{1,0:T(8,128)(2,1)S(1)}, u32[]{:S(2)}, u32[]{:S(2)}) %collective-permute-start.1) | collective-permute-done | bytes 262176 | tf_op jit(solution)/shard_map/ppermute | solution.py:100
  79.0 2.6 %collective-permute-done.refs_3_ = bf16[256,512]{1,0:T(8,128)(2,1)S(1)} collective-permute-done((bf16[256,512]{1,0:T(8,128)(2,1)S(1)}, bf16[256,512]{1,0:T(8,128)(2,1)S(1)}, u32[]{:S(2)}, u32[]{:S(2)}) %collective-permute-start) | collective-permute-done | bytes 262176 | tf_op jit(solution)/shard_map/ppermute | solution.py:100
  81.6 0.0 all-to-all-done.1
  81.6 0.0 copy-done.6
  81.6 0.0 copy-done.7
  81.6 0.0 copy-done.8
  81.6 0.0 copy-done.9
  81.6 0.0 copy-done.10
  81.6 0.7 copy-done.11
  82.3 0.3 copy-done.1
  82.6 41.4 %shard_map.75 = (bf16[256,2048]{1,0:T(8,128)(2,1)}, bf16[256,2048]{1,0:T(8,128)(2,1)}, bf16[256,512]{1,0:T(8,128)(2,1)}, bf16[256,512]{1,0:T(8,128)(2,1)}, bf16[...) custom-call(bf16[256,2048]{1,0:T(8,128)(2,1)} %bitcast.45, ...), custom_call_target="tpu_custom_call" | custom-call | tf_op jit(solution)/shard_map/pallas_call | solution.py:118
  124.1 1.9 collective-permute-start.6
  126.0 1.9 collective-permute-start.7
  127.9 1.9 collective-permute-start.8
  129.8 1.9 collective-permute-start.9
  131.8 1.9 collective-permute-start.10
  133.7 0.0 collective-permute-done.6
  133.7 1.3 collective-permute-start.11
  135.0 3.8 %collective-permute-done.7 = bf16[256,512]{1,0:T(8,128)(2,1)S(1)} collective-permute-done((bf16[256,512]{1,0:T(8,128)(2,1)}, bf16[256,512]{1,0:T(8,128)(2,1)S(1)}, u32[]{:S(2)}, u32[]{:S(2)}) %collective-permute-start.7) | collective-permute-done | bytes 262176 | tf_op jit(solution)/shard_map/ppermute | solution.py:100
  138.8 5.6 %collective-permute-done.8 = bf16[256,512]{1,0:T(8,128)(2,1)S(1)} collective-permute-done((bf16[256,512]{1,0:T(8,128)(2,1)}, bf16[256,512]{1,0:T(8,128)(2,1)S(1)}, u32[]{:S(2)}, u32[]{:S(2)}) %collective-permute-start.8) | collective-permute-done | bytes 262176 | tf_op jit(solution)/shard_map/ppermute | solution.py:100
  144.4 12.2 %collective-permute-done.9 = bf16[256,512]{1,0:T(8,128)(2,1)S(1)} collective-permute-done((bf16[256,512]{1,0:T(8,128)(2,1)}, bf16[256,512]{1,0:T(8,128)(2,1)S(1)}, u32[]{:S(2)}, u32[]{:S(2)}) %collective-permute-start.9) | collective-permute-done | bytes 262176 | tf_op jit(solution)/shard_map/ppermute | solution.py:100
  156.6 21.7 %collective-permute-done.10 = bf16[256,512]{1,0:T(8,128)(2,1)S(1)} collective-permute-done((bf16[256,512]{1,0:T(8,128)(2,1)}, bf16[256,512]{1,0:T(8,128)(2,1)S(1)}, u32[]{:S(2)}, u32[]{:S(2)}) %collective-permute-start.10) | collective-permute-done | bytes 262176 | tf_op jit(solution)/shard_map/ppermute | solution.py:100
  178.3 0.0 collective-permute-done.11
  178.3 1.3 add_convert_fusion
  179.6 11.0 %all_to_all.108 = bf16[4,64,512]{2,1,0:T(8,128)(2,1)S(1)} all-to-all(bf16[4,64,512]{2,1,0:T(8,128)(2,1)S(1)} %bitcast.53), channel_id=1, replica_groups=mesh['ctx'=64,'kvh'=4] {'kvh'}, dimensions={0} | all-to-all | bytes 524288 | tf_op jit(solution)/shard_map/all_to_all | solution.py:108
  190.6 0.0 copy-done.4
  190.6 15.6 %all_to_all.109 = bf16[4,64,2048]{2,1,0:T(8,128)(2,1)S(1)} all-to-all(bf16[4,64,2048]{2,1,0:T(8,128)(2,1)S(1)} %bitcast.49), channel_id=1, replica_groups=mesh['ctx'=64,'kvh'=4] {'kvh'}, dimensions={0} | all-to-all | bytes 2097152 | tf_op jit(solution)/shard_map/all_to_all | solution.py:108
  206.1 3.5 %all-to-all-start.3 = ((bf16[4,64,2048]{2,1,0:T(8,128)(2,1)}), bf16[4,64,2048]{2,1,0:T(8,128)(2,1)S(1)}, u32[]{:S(2)}, u32[]{:S(2)}) async-start(bf16[4,64,2048]{2,1,0:T(8,128)(2,1)} %bitcast.7), calls=%async_computation.3 | async-start | bytes 2097152 | tf_op jit(solution)/shard_map/all_to_all | solution.py:108
  209.6 0.1 reshape.40
  209.7 0.4 fusion
  210.1 0.2 copy.17
  210.3 0.7 copy.25
  210.9 0.2 copy.16
  211.1 0.7 copy.24
  211.8 1.0 copy.23
  212.8 8.8 %all-to-all-done.3 = bf16[4,64,2048]{2,1,0:T(8,128)(2,1)S(1)} async-done(((bf16[4,64,2048]{2,1,0:T(8,128)(2,1)}), bf16[4,64,2048]{2,1,0:T(8,128)(2,1)S(1)}, u32[]{:S(2)}, u32[]{:S(2)}) %all-to-all-start.3) | async-done | bytes 1048608 | tf_op jit(solution)/shard_map/all_to_all | solution.py:108
  221.6 1.0 copy.22
  (8 shorter events, 0.0 us)
Async XLA Ops:
  0.6 6.3 %copy-start.2 = (bf16[64,8192]{1,0:T(8,128)(2,1)S(1)}, bf16[64,8192]{1,0:T(8,128)(2,1)}, u32[]{:S(2)}) copy-start(bf16[64,8192]{1,0:T(8,128)(2,1)} %param.4) | copy-start | bytes 3145732
  2.4 11.1 %all-to-all-start.2 = ((bf16[64,4,512]{2,0,1:T(8,128)(2,1)}), bf16[64,4,512]{2,0,1:T(8,128)(2,1)S(1)}, u32[]{:S(2)}, u32[]{:S(2)}) async-start(bf16[64,4,512]{2,0,1:T(8,128)(2,1)} %pad_maximum_fusion), calls=%async_computation.2 | async-start | bytes 524288 | tf_op jit(solution)/shard_map/all_to_all | solution.py:104
  13.6 42.3 %copy-start.5 = (bf16[64,4,512]{2,0,1:T(8,128)(2,1)}, bf16[64,4,512]{2,0,1:T(8,128)(2,1)S(1)}, u32[]{:S(2)}) copy-start(bf16[64,4,512]{2,0,1:T(8,128)(2,1)S(1)} %all-to-all-done.2) | copy-start | bytes 786436
  13.6 3.7 %copy-start.3 = (bf16[64,8192]{1,0:T(8,128)(2,1)S(1)}, bf16[64,8192]{1,0:T(8,128)(2,1)}, u32[]{:S(2)}) copy-start(bf16[64,8192]{1,0:T(8,128)(2,1)} %param.7) | copy-start | bytes 3145732
  13.6 17.6 %all-to-all-start = ((bf16[64,4,2048]{2,0,1:T(8,128)(2,1)}), bf16[64,4,2048]{2,0,1:T(8,128)(2,1)S(1)}, u32[]{:S(2)}, u32[]{:S(2)}) async-start(bf16[64,4,2048]{2,0,1:T(8,128)(2,1)} %bitcast.42), calls=%async_computation | async-start | bytes 2097152 | tf_op jit(solution)/shard_map/all_to_all | solution.py:104
  31.2 1.0 copy-start
  32.2 49.4 %all-to-all-start.1 = ((bf16[64,4,2048]{2,0,1:T(8,128)(2,1)}), bf16[64,4,2048]{2,0,1:T(8,128)(2,1)S(1)}, u32[]{:S(2)}, u32[]{:S(2)}) async-start(bf16[64,4,2048]{2,0,1:T(8,128)(2,1)} %bitcast.41), calls=%async_computation.1 | async-start | bytes 2097152 | tf_op jit(solution)/shard_map/all_to_all | solution.py:104
  35.7 20.2 %collective-permute-start.5 = (bf16[256,512]{1,0:T(8,128)(2,1)S(1)}, bf16[256,512]{1,0:T(8,128)(2,1)S(1)}, u32[]{:S(2)}, u32[]{:S(2)}) collective-permute-start(bf16[256,512]{1,0:T(8,128)(2,1)S(1)} %bitcast.54), channel_id=1, source_target_pairs={{0,128},{4,132},{8,136},{12,140},{16,144},{20,148},{24,152},{28,15... | collective-permute-start | bytes 786440 | tf_op jit(solution)/shard_map/ppermute | solution.py:100
  43.0 21.2 %collective-permute-start.4 = (bf16[256,512]{1,0:T(8,128)(2,1)S(1)}, bf16[256,512]{1,0:T(8,128)(2,1)S(1)}, u32[]{:S(2)}, u32[]{:S(2)}) collective-permute-start(bf16[256,512]{1,0:T(8,128)(2,1)S(1)} %bitcast.55), channel_id=1, source_target_pairs={{0,64},{4,68},{8,72},{12,76},{16,80},{20,84},{24,88},{28,92},{32,9... | collective-permute-start | bytes 786440 | tf_op jit(solution)/shard_map/ppermute | solution.py:100
  44.9 23.9 %collective-permute-start.3 = (bf16[256,512]{1,0:T(8,128)(2,1)S(1)}, bf16[256,512]{1,0:T(8,128)(2,1)S(1)}, u32[]{:S(2)}, u32[]{:S(2)}) collective-permute-start(bf16[256,512]{1,0:T(8,128)(2,1)S(1)} %bitcast.56), channel_id=1, source_target_pairs={{0,32},{4,36},{8,40},{12,44},{16,48},{20,52},{24,56},{28,60},{32,6... | collective-permute-start | bytes 786440 | tf_op jit(solution)/shard_map/ppermute | solution.py:100
  47.9 25.6 %collective-permute-start.2 = (bf16[256,512]{1,0:T(8,128)(2,1)S(1)}, bf16[256,512]{1,0:T(8,128)(2,1)S(1)}, u32[]{:S(2)}, u32[]{:S(2)}) collective-permute-start(bf16[256,512]{1,0:T(8,128)(2,1)S(1)} %bitcast.57), channel_id=1, source_target_pairs={{0,16},{4,20},{8,24},{12,28},{16,32},{20,36},{24,40},{28,44},{32,4... | collective-permute-start | bytes 786440 | tf_op jit(solution)/shard_map/ppermute | solution.py:100
  52.8 26.2 %collective-permute-start.1 = (bf16[256,512]{1,0:T(8,128)(2,1)S(1)}, bf16[256,512]{1,0:T(8,128)(2,1)S(1)}, u32[]{:S(2)}, u32[]{:S(2)}) collective-permute-start(bf16[256,512]{1,0:T(8,128)(2,1)S(1)} %bitcast.58), channel_id=1, source_target_pairs={{0,8},{4,12},{8,16},{12,20},{16,24},{20,28},{24,32},{28,36},{32,40... | collective-permute-start | bytes 786440 | tf_op jit(solution)/shard_map/ppermute | solution.py:100
  55.8 25.8 %copy-start.6 = (bf16[256,512]{1,0:T(8,128)(2,1)}, bf16[256,512]{1,0:T(8,128)(2,1)S(1)}, u32[]{:S(2)}) copy-start(bf16[256,512]{1,0:T(8,128)(2,1)S(1)} %collective-permute-done.5.refs_8_) | copy-start | bytes 786436
  55.8 25.7 %collective-permute-start = (bf16[256,512]{1,0:T(8,128)(2,1)S(1)}, bf16[256,512]{1,0:T(8,128)(2,1)S(1)}, u32[]{:S(2)}, u32[]{:S(2)}) collective-permute-start(bf16[256,512]{1,0:T(8,128)(2,1)S(1)} %bitcast.59), channel_id=1, source_target_pairs={{0,4},{4,8},{8,12},{12,16},{16,20},{20,24},{24,28},{28,32},{32,36}... | collective-permute-start | bytes 786440 | tf_op jit(solution)/shard_map/ppermute | solution.py:100
  64.2 17.4 %copy-start.7 = (bf16[256,512]{1,0:T(8,128)(2,1)}, bf16[256,512]{1,0:T(8,128)(2,1)S(1)}, u32[]{:S(2)}) copy-start(bf16[256,512]{1,0:T(8,128)(2,1)S(1)} %collective-permute-done.4.refs_7_) | copy-start | bytes 786436
  68.8 12.8 %copy-start.8 = (bf16[256,512]{1,0:T(8,128)(2,1)}, bf16[256,512]{1,0:T(8,128)(2,1)S(1)}, u32[]{:S(2)}) copy-start(bf16[256,512]{1,0:T(8,128)(2,1)S(1)} %collective-permute-done.3.refs_6_) | copy-start | bytes 786436
  73.4 8.2 %copy-start.9 = (bf16[256,512]{1,0:T(8,128)(2,1)}, bf16[256,512]{1,0:T(8,128)(2,1)S(1)}, u32[]{:S(2)}) copy-start(bf16[256,512]{1,0:T(8,128)(2,1)S(1)} %collective-permute-done.2.refs_5_) | copy-start | bytes 786436
  79.0 2.6 %copy-start.10 = (bf16[256,512]{1,0:T(8,128)(2,1)}, bf16[256,512]{1,0:T(8,128)(2,1)S(1)}, u32[]{:S(2)}) copy-start(bf16[256,512]{1,0:T(8,128)(2,1)S(1)} %collective-permute-done.1.refs_4_) | copy-start | bytes 786436
  81.6 0.7 copy-start.11
  81.6 1.1 copy-start.1
  124.1 9.6 %collective-permute-start.6 = (bf16[256,512]{1,0:T(8,128)(2,1)}, bf16[256,512]{1,0:T(8,128)(2,1)S(1)}, u32[]{:S(2)}, u32[]{:S(2)}) collective-permute-start(bf16[256,512]{1,0:T(8,128)(2,1)} %get-tuple-element.16), channel_id=1, source_target_pairs={{4,0},{8,4},{12,8},{16,12},{20,16},{24,20},{28,24},{32,28},{36,32}... | collective-permute-start | bytes 786440 | tf_op jit(solution)/shard_map/ppermute | solution.py:100
  126.0 12.8 %collective-permute-start.7 = (bf16[256,512]{1,0:T(8,128)(2,1)}, bf16[256,512]{1,0:T(8,128)(2,1)S(1)}, u32[]{:S(2)}, u32[]{:S(2)}) collective-permute-start(bf16[256,512]{1,0:T(8,128)(2,1)} %get-tuple-element.17), channel_id=1, source_target_pairs={{8,0},{12,4},{16,8},{20,12},{24,16},{28,20},{32,24},{36,28},{40,32... | collective-permute-start | bytes 786440 | tf_op jit(solution)/shard_map/ppermute | solution.py:100
  127.9 16.5 %collective-permute-start.8 = (bf16[256,512]{1,0:T(8,128)(2,1)}, bf16[256,512]{1,0:T(8,128)(2,1)S(1)}, u32[]{:S(2)}, u32[]{:S(2)}) collective-permute-start(bf16[256,512]{1,0:T(8,128)(2,1)} %get-tuple-element.18), channel_id=1, source_target_pairs={{16,0},{20,4},{24,8},{28,12},{32,16},{36,20},{40,24},{44,28},{48,3... | collective-permute-start | bytes 786440 | tf_op jit(solution)/shard_map/ppermute | solution.py:100
  129.8 26.8 %collective-permute-start.9 = (bf16[256,512]{1,0:T(8,128)(2,1)}, bf16[256,512]{1,0:T(8,128)(2,1)S(1)}, u32[]{:S(2)}, u32[]{:S(2)}) collective-permute-start(bf16[256,512]{1,0:T(8,128)(2,1)} %get-tuple-element.19), channel_id=1, source_target_pairs={{32,0},{36,4},{40,8},{44,12},{48,16},{52,20},{56,24},{60,28},{64,3... | collective-permute-start | bytes 786440 | tf_op jit(solution)/shard_map/ppermute | solution.py:100
  131.8 46.6 %collective-permute-start.10 = (bf16[256,512]{1,0:T(8,128)(2,1)}, bf16[256,512]{1,0:T(8,128)(2,1)S(1)}, u32[]{:S(2)}, u32[]{:S(2)}) collective-permute-start(bf16[256,512]{1,0:T(8,128)(2,1)} %get-tuple-element.20), channel_id=1, source_target_pairs={{64,0},{68,4},{72,8},{76,12},{80,16},{84,20},{88,24},{92,28},{96,3... | collective-permute-start | bytes 786440 | tf_op jit(solution)/shard_map/ppermute | solution.py:100
  133.7 44.6 %collective-permute-start.11 = (bf16[256,512]{1,0:T(8,128)(2,1)}, bf16[256,512]{1,0:T(8,128)(2,1)S(1)}, u32[]{:S(2)}, u32[]{:S(2)}) collective-permute-start(bf16[256,512]{1,0:T(8,128)(2,1)} %get-tuple-element.21), channel_id=1, source_target_pairs={{128,0},{132,4},{136,8},{140,12},{144,16},{148,20},{152,24},{156,2... | collective-permute-start | bytes 786440 | tf_op jit(solution)/shard_map/ppermute | solution.py:100
  178.3 12.2 %copy-start.4 = (bf16[256,2048]{1,0:T(8,128)(2,1)S(1)}, bf16[256,2048]{1,0:T(8,128)(2,1)}, u32[]{:S(2)}) copy-start(bf16[256,2048]{1,0:T(8,128)(2,1)} %get-tuple-element.14) | copy-start | bytes 3145732
  206.1 15.5 %all-to-all-start.3 = ((bf16[4,64,2048]{2,1,0:T(8,128)(2,1)}), bf16[4,64,2048]{2,1,0:T(8,128)(2,1)S(1)}, u32[]{:S(2)}, u32[]{:S(2)}) async-start(bf16[4,64,2048]{2,1,0:T(8,128)(2,1)} %bitcast.7), calls=%async_computation.3 | async-start | bytes 2097152 | tf_op jit(solution)/shard_map/all_to_all | solution.py:108
where the time goes:
time: 223 us
  waiting for transfers between devices  95 us (43%)
  starting transfers between devices  47.5 us (21%)
  Pallas kernels  41.4 us (19%)
  blocking collectives  26.5 us (12%)
  local copies, waits for them, and re-layouts  9.35 us (4%)
    ppermute x12, waiting for transfers between devices, shifted(): lax.ppermute(array, 'ctx', [(i, i + by) for i in range(peers) if 0 <= i +...  67.7 us
    pallas_call x1, Pallas kernels, shards(): pl.pallas_call(kernel, out_shape=(jax.ShapeDtypeStruct((BLK, GRP * QPK *...  41.4 us
    ppermute x12, starting transfers between devices, shifted(): lax.ppermute(array, 'ctx', [(i, i + by) for i in range(peers) if 0 <= i +...  32.4 us
    all_to_all x2, blocking collectives, a2a_out(): return lax.all_to_all(x, 'kvh', split_axis=0, concat_axis=1, tiled=True)  26.5 us
    all_to_all x3, waiting for transfers between devices, a2a_in(): return lax.all_to_all(x, 'kvh', split_axis=1, concat_axis=0, tiled=True)  18.5 us
    all_to_all x3, starting transfers between devices, a2a_in(): return lax.all_to_all(x, 'kvh', split_axis=1, concat_axis=0, tiled=True)  11.6 us
    all_to_all x1, waiting for transfers between devices, a2a_out(): return lax.all_to_all(x, 'kvh', split_axis=0, concat_axis=1, tiled=True)  8.79 us
  transfers between devices with their start and end apart: 16, of which 13 were waited for; matrix products, arithmetic and copies ran while one was open for 2% of the time, Pallas kernels for 0%

commit v1 on v0

v1 whole, which is shorter than its diff:
```python
import jax
import jax.numpy as jnp
from jax import lax
from jax.experimental import pallas as pl
from jax.experimental.pallas import tpu as pltpu
from jax.sharding import PartitionSpec as P

HD = 128
QPK = 8
BLK = 256
NL = 7
GRP = 2
NKV = 4
NCTX = 64
TOK = BLK // NKV
CH = 2
NCH = GRP * QPK // CH
CW = CH * HD
QW = GRP * QPK * HD
KW = GRP * HD
SCALE = HD**-0.5
C2 = SCALE * 1.4426950408889634
F32 = jnp.float32
BF = jnp.bfloat16
MESH = pl.DeviceIdType.MESH
ctx_offsets = (1, 2, 4, 6, 7, 8, 16, 32, 48, 56, 57, 58, 60, 62, 63)


def nt(a, b):
    return lax.dot_general(a, b, (((1,), (1,)), ((), ())), preferred_element_type=F32)


def nn(a, b):
    return lax.dot_general(a, b, (((1,), (0,)), ((), ())), preferred_element_type=F32)


def head(g, r, valid, qbuf, gbuf, kvb, ktb, vtb, outb, gqb, s_scr, dp_scr, p_scr, ds_scr, gs_scr, qs_scr):
    col = pl.multiple_of((g * QPK + r) * HD, HD)
    row = pl.multiple_of(r * BLK, BLK)
    q = qbuf[:, pl.ds(col, HD)]
    go = gbuf[:, pl.ds(col, HD)]
    top = None
    for j in range(NL):
        s = nt(kvb[g, j, :, :HD], q)
        dp_scr[j] = nt(kvb[g, j, :, HD:], go)
        if j == 0:
            u = lax.broadcasted_iota(jnp.int32, (BLK, BLK), 0)
            t = lax.broadcasted_iota(jnp.int32, (BLK, BLK), 1)
            s = jnp.where(u <= t, s, -1e30)
        s_scr[j] = s
        mj = jnp.max(s, axis=0, keepdims=True)
        top = mj if j == 0 else jnp.maximum(top, jnp.where(valid[j], mj, -1e30))
    total = jnp.zeros((1, BLK), F32)
    acc = jnp.zeros((HD, BLK), F32)
    for j in range(NL):
        sub = top if j == 0 else jnp.where(valid[j], top, 1e30)
        p = jnp.exp2((s_scr[j] - sub) * C2)
        s_scr[j] = p
        total = total + jnp.sum(p, axis=0, keepdims=True)
        pb = p.astype(BF)
        p_scr[j, :, pl.ds(row, BLK)] = pb
        acc = acc + nn(vtb[g, j], pb)
    inv = 1.0 / total
    ot = (acc * inv).astype(BF)
    outb[:, pl.ds(col, HD)] = ot.T
    delta = jnp.sum(ot.astype(F32) * go.T.astype(F32), axis=0, keepdims=True)
    acc = jnp.zeros((HD, BLK), F32)
    for j in range(NL):
        ds = (s_scr[j] * (dp_scr[j] - delta)).astype(BF)
        ds_scr[j, :, pl.ds(row, BLK)] = ds
        acc = acc + nn(ktb[g, j], ds)
    gqb[:, pl.ds(col, HD)] = (acc * (inv * SCALE)).astype(BF).T
    invb = jnp.broadcast_to(inv, (HD, BLK)).T
    gs_scr[pl.ds(row, BLK), :] = (go.astype(F32) * invb).astype(BF)
    qs_scr[pl.ds(row, BLK), :] = (q.astype(F32) * (invb * SCALE)).astype(BF)


def kernel(
    q_in, k_in, v_in, g_in,
    out_o, gq_o, gk_o, gv_o,
    qbuf, gbuf, kvb, ktb, vtb, outb, gqb,
    s_scr, dp_scr, p_scr, ds_scr, gs_scr, qs_scr,
    gsend, grecv, own, part8, gfin,
    loc_sem, in_ss, in_rs, kv_ss, kv_rs, ring_ss, ring_rs, gr_ss, gr_rs, out_ss, out_rs, out_loc, fin_ss, fin_rs, fin_loc,
):
    c = lax.axis_index("ctx")
    h = lax.axis_index("kvh")
    low = lax.rem(c, 8)
    valid = [None] + [c >= 1 << j for j in range(NL - 1)]
    mine = pl.ds(pl.multiple_of(h * TOK, TOK), TOK)

    local = [
        pltpu.make_async_copy(q_in.at[:, pl.ds(pl.multiple_of(h * QW, QW), QW)], qbuf.at[mine], loc_sem.at[0]),
        pltpu.make_async_copy(g_in.at[:, pl.ds(pl.multiple_of(h * QW, QW), QW)], gbuf.at[mine], loc_sem.at[1]),
    ]
    for g in range(GRP):
        src = pl.ds(pl.multiple_of(h * KW + g * HD, HD), HD)
        local.append(pltpu.make_async_copy(k_in.at[:, src], kvb.at[g, 0, mine, pl.ds(0, HD)], loc_sem.at[2 + 2 * g]))
        local.append(pltpu.make_async_copy(v_in.at[:, src], kvb.at[g, 0, mine, pl.ds(HD, HD)], loc_sem.at[3 + 2 * g]))
    for cp in local:
        cp.start()
    for j in range(1, NL):
        @pl.when(jnp.logical_not(valid[j]))
        def _():
            for g in range(GRP):
                kvb[g, j] = jnp.zeros((BLK, 2 * HD), BF)

    bar = pltpu.get_barrier_semaphore()
    for o in range(1, NKV):
        pl.semaphore_signal(bar, 1, device_id={"kvh": lax.rem(h + o, NKV)}, device_id_type=MESH)
    for o in ctx_offsets:
        pl.semaphore_signal(bar, 1, device_id={"ctx": lax.rem(c + o, NCTX)}, device_id_type=MESH)
    pl.semaphore_wait(bar, NKV - 1 + len(ctx_offsets))

    def kv_copy(g, a, o):
        p = lax.rem(h + o, NKV)
        ref = (k_in, v_in)[a]
        return pltpu.make_async_remote_copy(
            ref.at[:, pl.ds(pl.multiple_of(p * KW + g * HD, HD), HD)],
            kvb.at[g, 0, mine, pl.ds(a * HD, HD)],
            kv_ss.at[g, a, o - 1], kv_rs.at[g, a, o - 1],
            device_id={"kvh": p}, device_id_type=MESH,
        )

    def in_copy(k, a, o):
        p = lax.rem(h + o, NKV)
        ref, buf = ((q_in, qbuf), (g_in, gbuf))[a]
        return pltpu.make_async_remote_copy(
            ref.at[:, pl.ds(pl.multiple_of(p * QW + k * CW, CW), CW)],
            buf.at[mine, pl.ds(pl.multiple_of(k * CW, CW), CW)],
            in_ss.at[k, a, o - 1], in_rs.at[k, a, o - 1],
            device_id={"kvh": p}, device_id_type=MESH,
        )

    def out_copy(k, a, o):
        p = lax.rem(h + o, NKV)
        buf, ref = ((outb, out_o), (gqb, gq_o))[a]
        return pltpu.make_async_remote_copy(
            buf.at[pl.ds(pl.multiple_of(p * TOK, TOK), TOK), pl.ds(pl.multiple_of(k * CW, CW), CW)],
            ref.at[:, pl.ds(pl.multiple_of(h * QW + k * CW, CW), CW)],
            out_ss.at[k, a, o - 1], out_rs.at[k, a, o - 1],
            device_id={"kvh": p}, device_id_type=MESH,
        )

    def out_local(k, a):
        buf, ref = ((outb, out_o), (gqb, gq_o))[a]
        return pltpu.make_async_copy(
            buf.at[mine, pl.ds(pl.multiple_of(k * CW, CW), CW)],
            ref.at[:, pl.ds(pl.multiple_of(h * QW + k * CW, CW), CW)],
            out_loc.at[k, a],
        )

    def fin_copy(g, a, o):
        p = lax.rem(h + o, NKV)
        return pltpu.make_async_remote_copy(
            gfin.at[g, pl.ds(pl.multiple_of(p * TOK, TOK), TOK), pl.ds(a * HD, HD)],
            (gk_o, gv_o)[a].at[:, pl.ds(pl.multiple_of(h * KW + g * HD, HD), HD)],
            fin_ss.at[g, a, o - 1], fin_rs.at[g, a, o - 1],
            device_id={"kvh": p}, device_id_type=MESH,
        )

    def fin_local(g, a):
        return pltpu.make_async_copy(
            gfin.at[g, mine, pl.ds(a * HD, HD)],
            (gk_o, gv_o)[a].at[:, pl.ds(pl.multiple_of(h * KW + g * HD, HD), HD)],
            fin_loc.at[g, a],
        )

    def ring(g, j, from8):
        src, at = (4, c - 8) if from8 else (0, c)
        return pltpu.make_async_remote_copy(
            kvb.at[g, src], kvb.at[g, j], ring_ss.at[g, j], ring_rs.at[g, j],
            device_id={"ctx": at + (1 << (j - 1))}, device_id_type=MESH,
        )

    def send_own(g):
        for j in (4, 2, 6, 3, 1):
            d = 1 << (j - 1)
            cond = c + d < NCTX if j >= 4 else low + d < 8

            @pl.when(cond)
            def _():
                ring(g, j, False).start()

    def forward(g):
        @pl.when(c >= 8)
        def _():
            ring(g, 4, False).wait_recv()
            for j in (5, 2, 3, 1):
                d = 1 << (j - 1)

                @pl.when(c + 8 < NCTX if j == 5 else low + d >= 8)
                def _():
                    ring(g, j, True).start()

    def term(g, j):
        d = 1 << (j - 1)
        if j in (4, 6):
            dest = c - d
        elif j == 5:
            dest = c - 8
        else:
            dest = jnp.where(low >= d, c - d, c - d + 8)
        return pltpu.make_async_remote_copy(
            gsend.at[g, j], grecv.at[g, j], gr_ss.at[g, j], gr_rs.at[g, j],
            device_id={"ctx": dest}, device_id_type=MESH,
        )

    for g in range(GRP):
        for o in (1, 3, 2):
            for a in range(2):
                kv_copy(g, a, o).start()

    def send_in(k, _):
        for a in range(2):
            for o in (1, 3, 2):
                in_copy(k, a, o).start()
        return 0

    lax.fori_loop(0, NCH, send_in, 0)
    for cp in local[2:]:
        cp.wait()
    for g in range(GRP):
        for o in (1, 3, 2):
            for a in range(2):
                kv_copy(g, a, o).wait_recv()
        send_own(g)
    for g in range(GRP):
        forward(g)
    for cp in local[:2]:
        cp.wait()

    def relay(g):
        t8 = part8[g]
        pick = [(5, jnp.logical_and(c >= 8, c + 8 < NCTX))]
        for j in (1, 2, 3):
            pick.append((j, jnp.logical_and(c >= 8, low + (1 << (j - 1)) >= 8)))
        part8[g] = t8
        for j, cond in pick:
            @pl.when(cond)
            def _():
                term(g, j).wait_recv()
                part8[g] = part8[g] + grecv[g, j].astype(F32)
        gsend[g, 4] = part8[g].astype(BF)

        @pl.when(c >= 8)
        def _():
            term(g, 4).start()

    def finish(g):
        pick = [(6, c + 32 < NCTX), (4, c + 8 < NCTX)]
        for j in (1, 2, 3):
            pick.append((j, low + (1 << (j - 1)) < 8))
        for j, cond in pick:
            @pl.when(cond)
            def _():
                term(g, j).wait_recv()
                own[g] = own[g] + grecv[g, j].astype(F32)
        gfin[g] = own[g].astype(BF)
        for a in range(2):
            for o in (1, 3, 2):
                fin_copy(g, a, o).start()
            fin_local(g, a).start()

    def group(g, _):
        for j in (1, 2, 3, 5, 6):
            @pl.when(valid[j])
            def _():
                ring(g, j, False).wait_recv()
        for j in range(NL):
            ktb[g, j] = kvb[g, j, :, :HD].T
            vtb[g, j] = kvb[g, j, :, HD:].T

        def body(r, _):
            k = g * (QPK // CH) + r // CH

            @pl.when(lax.rem(r, CH) == 0)
            def _():
                for a in range(2):
                    for o in range(1, NKV):
                        in_copy(k, a, o).wait_recv()

            head(g, r, valid, qbuf, gbuf, kvb, ktb, vtb, outb, gqb, s_scr, dp_scr, p_scr, ds_scr, gs_scr, qs_scr)

            @pl.when(lax.rem(r, CH) == CH - 1)
            def _():
                for a in range(2):
                    for o in (1, 3, 2):
                        out_copy(k, a, o).start()
                    out_local(k, a).start()

            @pl.when(jnp.logical_and(g == 1, r == 1))
            def _():
                relay(0)

            @pl.when(jnp.logical_and(g == 1, r == 4))
            def _():
                finish(0)

            return 0

        lax.fori_loop(0, QPK, body, 0)
        for j in (5, 3, 2, 1, 6, 4, 0):
            gk = nn(ds_scr[j], qs_scr[...])
            gv = nn(p_scr[j], gs_scr[...])
            if j in (0, 4):
                acc = own if j == 0 else part8
                acc[g, :, :HD] = gk
                acc[g, :, HD:] = gv
            else:
                gsend[g, j, :, :HD] = gk.astype(BF)
                gsend[g, j, :, HD:] = gv.astype(BF)

                @pl.when(valid[j])
                def _():
                    term(g, j).start()

        return 0

    lax.fori_loop(0, GRP, group, 0)
    relay(1)
    finish(1)

    def drain(k, _):
        for a in range(2):
            for o in range(1, NKV):
                in_copy(k, a, o).wait_send()
                out_copy(k, a, o).wait()
            out_local(k, a).wait()
        return 0

    lax.fori_loop(0, NCH, drain, 0)
    for g in range(GRP):
        for a in range(2):
            for o in range(1, NKV):
                kv_copy(g, a, o).wait_send()
                fin_copy(g, a, o).wait()
            fin_local(g, a).wait()
        for j in range(1, NL):
            d = 1 << (j - 1)
            if j in (4, 6):
                cond = c + d < NCTX
            elif j == 5:
                cond = jnp.logical_and(c >= 8, c + 8 < NCTX)
            else:
                cond = jnp.logical_or(low + d < 8, c >= 8)

            @pl.when(cond)
            def _():
                ring(g, j, False).wait_send()

            @pl.when(valid[j])
            def _():
                term(g, j).wait_send()


def shards(query_act, key_act, value_act, grad_out):
    hbm = pl.BlockSpec(memory_space=pl.ANY)
    dma = pltpu.SemaphoreType.DMA
    return tuple(
        pl.pallas_call(
            kernel,
            out_shape=tuple(jax.ShapeDtypeStruct(a.shape, BF) for a in (query_act, query_act, key_act, value_act)),
            in_specs=[hbm] * 4,
            out_specs=(hbm,) * 4,
            scratch_shapes=[pltpu.VMEM((BLK, QW), BF)] * 2
            + [pltpu.VMEM((GRP, NL, BLK, 2 * HD), BF)]
            + [pltpu.VMEM((GRP, NL, HD, BLK), BF)] * 2
            + [pltpu.VMEM((BLK, QW), BF)] * 2
            + [pltpu.VMEM((NL, BLK, BLK), F32)] * 2
            + [pltpu.VMEM((NL, BLK, QPK * BLK), BF)] * 2
            + [pltpu.VMEM((QPK * BLK, HD), BF)] * 2
            + [pltpu.VMEM((GRP, NL, BLK, 2 * HD), BF)] * 2
            + [pltpu.VMEM((GRP, BLK, 2 * HD), F32)] * 2
            + [pltpu.VMEM((GRP, BLK, 2 * HD), BF)]
            + [dma((6,))]
            + [dma((NCH, 2, 3))] * 2
            + [dma((GRP, 2, 3))] * 2
            + [dma((GRP, NL))] * 4
            + [dma((NCH, 2, 3))] * 2
            + [dma((NCH, 2))]
            + [dma((GRP, 2, 3))] * 2
            + [dma((GRP, 2))],
            compiler_params=pltpu.CompilerParams(
                vmem_limit_bytes=60 * 2**20, collective_id=0, has_side_effects=True
            ),
        )(query_act, key_act, value_act, grad_out)
    )


def solution(mesh):
    spec = P(("ctx", "kvh"), None)
    return jax.shard_map(shards, mesh=mesh, in_specs=(spec,) * 4, out_specs=(spec,) * 4, check_vma=False)
```

time: 223 us -> 99.3 us (0.45)
  waiting for transfers between devices: 95 us -> 0 us
  Pallas kernels: 41.4 us -> 93 us
  starting transfers between devices: 47.5 us -> 0 us
  blocking collectives: 26.5 us -> 0 us
  local copies, waits for them, and re-layouts: 9.35 us -> 4.98 us
    ppermute x12 -> x0, waiting for transfers between devices: 67.7 us -> none  [shifted(): lax.ppermute(array, 'ctx', [(i, i + by) for i in range(peers) if 0 <= i +...]
    pallas_call x1, Pallas kernels: 41.4 us -> 93 us  [shards(): pl.pallas_call(kernel, out_shape=tuple((jax.ShapeDtypeStruct(a.shape, BF)...]
    ppermute x12 -> x0, starting transfers between devices: 32.4 us -> none  [shifted(): lax.ppermute(array, 'ctx', [(i, i + by) for i in range(peers) if 0 <= i +...]
    all_to_all x4 -> x0, waiting for transfers between devices: 27.3 us -> none  [the longest x3 18.5 us: a2a_in(): return lax.all_to_all(x, 'kvh', split_axis=1, concat_axis=0, tiled=True)]
    all_to_all x2 -> x0, blocking collectives: 26.5 us -> none  [a2a_out(): return lax.all_to_all(x, 'kvh', split_axis=0, concat_axis=1, tiled=True)]
    all_to_all x4 -> x0, starting transfers between devices: 15.1 us -> none  [the longest x3 11.6 us: a2a_in(): return lax.all_to_all(x, 'kvh', split_axis=1, concat_axis=0, tiled=True)]
    all_to_all x4 -> x0, local copies, waits for them, and re-layouts: 4.15 us -> none  [the longest x2 2.08 us: a2a_in(): return lax.all_to_all(x, 'kvh', split_axis=1, concat_axis=0, tiled=True)]
    unnamed x28 -> x10, local copies, waits for them, and re-layouts: 3.7 us -> 4.98 us
  transfers between devices with their start and end apart: 16 -> 0, of which waited for: 13 -> 0; matrix products, arithmetic and copies ran while one was open for 2% -> 0% of each run, Pallas kernels for 0% -> 0%
where the time goes in v1:
time: 99.3 us; the launch traced here: 98.6 us
  Pallas kernels  93 us (94%)
  local copies, waits for them, and re-layouts  4.98 us (5%)
    pallas_call x1, Pallas kernels, shards(): pl.pallas_call(kernel, out_shape=tuple((jax.ShapeDtypeStruct(a.shape, BF)...  93 us
    unnamed x10, local copies, waits for them, and re-layouts  4.98 us

profile of v1, /device:TPU:64, one launch (start us, length us, event | category | flops | bytes accessed | tf_op | source)
XLA Modules:
  0.0 98.6 jit_solution(12055333920146348603)
XLA Ops:
  0.6 93.0 %shard_map.75 = (bf16[64,8192]{1,0:T(8,128)(2,1)}, bf16[64,8192]{1,0:T(8,128)(2,1)}, bf16[64,1024]{1,0:T(8,128)(2,1)}, bf16[64,1024]{1,0:T(8,128)(2,1)}) custom-call(bf16[64,8192]{1,0:T(8,128)(2,1)} %q_in.1, bf16[64,1024]{1,0:T(8,128)(2,1)} %k_in.1, bf16[64,1024]{1,0:T(8,128)(2,1)} %v_in.1, bf16[64,8192]{1,0:T(8,128)(2,1)} %g_in.1), custom_call_target="tpu_custom_call" | custom-call | tf_op jit(solution)/shard_map/pallas_call | solution.py:361
  93.6 0.0 copy-start
  93.6 2.4 %copy.12 = bf16[64,8192]{1,0:T(8,128)(2,1)} copy(bf16[64,8192]{1,0:T(8,128)(2,1)} %get-tuple-element.8) | data formatting | bytes 2097152
  96.0 0.0 copy-done
  96.0 0.0 copy-start.2
  96.0 1.0 copy.13
  96.9 0.1 copy-done.2
  97.0 0.0 copy-start.1
  97.0 0.7 copy.14
  97.6 0.3 copy-done.1
  97.9 0.7 copy.15
Async XLA Ops:
  93.6 2.4 %copy-start = (bf16[64,8192]{1,0:T(8,128)(2,1)S(1)}, bf16[64,8192]{1,0:T(8,128)(2,1)}, u32[]{:S(2)}) copy-start(bf16[64,8192]{1,0:T(8,128)(2,1)} %get-tuple-element.9) | copy-start | bytes 3145732
  96.0 1.0 %copy-start.2 = (bf16[64,1024]{1,0:T(8,128)(2,1)S(1)}, bf16[64,1024]{1,0:T(8,128)(2,1)}, u32[]{:S(2)}) copy-start(bf16[64,1024]{1,0:T(8,128)(2,1)} %get-tuple-element.10) | copy-start | bytes 393220
  97.0 1.0 copy-start.1
